TPU v7x, 32 devices: a whole 2x2x4 slice. The times are simulated.
32 devices in a mesh: slide: 4 (over x, core), rows: 8 (over z, y).
Axes of the slice: x: 2, y: 2, z: 4, core: 2. Of those that a mesh axis runs over, the one named last changes fastest.
Arguments:
- features: bfloat16 [4, 192, 256, 128], P('slide', None, 'rows'), may hold values from -6 to 6
- depth_kernel: float32 [192, 49], replicated, may hold values from -0.875 to 0.875
- depth_bias: float32 [192], replicated, may hold values from -4 to 4
- norm_gain: float32 [192], replicated, may hold values from 0.1 to 1.9
- norm_bias: float32 [192], replicated, may hold values from -3 to 3
- up_weight: bfloat16 [192, 768], replicated, may hold values from -0.4375 to 0.4375
- up_bias: float32 [768], replicated, may hold values from -3 to 3
- down_weight: bfloat16 [768, 192], replicated, may hold values from -0.21875 to 0.21875
- down_bias: float32 [192], replicated, may hold values from -4 to 4
- layer_scale: float32 [192], replicated, may hold values from 0.2 to 1
- tissue: int32 [4, 8, 4], P('slide', 'rows'), may hold values 0 or 1
- aggregator_order: int32 [4, 32], P('slide'), may hold values from 0 to 31, each once within a row
- tile_cotangent: bfloat16 [4, 32, 192], P('slide', 'rows'), may hold values from -6 to 6
Outputs:
- embedding: float32 [4, 32, 192], P('slide', 'rows')
- input_grad: bfloat16 [4, 192, 256, 128], P('slide', None, 'rows')
- grad_up: float32 [192, 768], replicated
- grad_down: float32 [768, 192], replicated
- grad_kernel: float32 [192, 49], replicated
Inputs may be any that keep to these rules, and one draw needn't show every extreme that they name: `aggregator_order`: each slide's row is a permutation of the 32 positions.
All inputs are finite; a program needn't handle non-finite values. No bound on the sum of `tissue` on one device may be relied on, other than what follows from the above.
Results may differ from a plain program's by a relative error of at most 0.0064.
Values may be sent and summed in bfloat16 or wider, within the bound.
A program may use at most 128 MiB of HBM per device.

v0:
```python
import functools
import math

import jax
import jax.numpy as jnp
import numpy as np
from jax import lax
from jax.experimental import pallas as pl
from jax.experimental.pallas import tpu as pltpu
from jax.sharding import PartitionSpec as P

TILE = 32
SLOT = 40
PER = 3
ROWS = 4
MESH = pl.DeviceIdType.MESH
VMEM = pl.BlockSpec(memory_space=pltpu.VMEM)


def greet(peers):
    barrier = pltpu.get_barrier_semaphore()
    for peer in peers:
        pl.semaphore_signal(barrier, inc=1, device_id=peer, device_id_type=MESH)
    pl.semaphore_wait(barrier, len(peers))


def remote(source, target, send, receive, peer, start=True):
    copy = pltpu.make_async_remote_copy(
        src_ref=source,
        dst_ref=target,
        send_sem=send,
        recv_sem=receive,
        device_id=peer,
        device_id_type=MESH,
    )
    if start:
        copy.start()
    return copy


def halo_kernel(count, gathers, head_ref, tail_ref, *refs):
    if gathers:
        block_ref, above_ref, below_ref, all_ref, edge_send, edge_recv, send, recv, own = refs
    else:
        above_ref, below_ref, edge_send, edge_recv = refs
    slide, me = lax.axis_index("slide"), lax.axis_index("rows")
    peers = [(slide, lax.rem(me + k, count)) for k in range(1, count)]
    up, down = peers[-1], peers[0]
    has_up, has_down = me > 0, me < count - 1
    greet(peers if gathers else [up, down])
    downward = remote(tail_ref, above_ref, edge_send.at[0], edge_recv.at[0], down, False)
    upward = remote(head_ref, below_ref, edge_send.at[1], edge_recv.at[1], up, False)
    pl.when(has_down)(downward.start)
    pl.when(has_up)(upward.start)
    if gathers:
        copies = [
            remote(block_ref, all_ref.at[me], send.at[k], recv.at[k], peers[k - 1])
            for k in range(1, count)
        ]
        mine = pltpu.make_async_copy(block_ref, all_ref.at[me], own)
        mine.start()
        mine.wait()
        for copy in copies:
            copy.wait()
    pl.when(has_down)(downward.wait_send)
    pl.when(has_up)(upward.wait_send)
    pl.when(has_up)(downward.wait_recv)
    pl.when(has_down)(upward.wait_recv)


def halo(cells, count, channel_id, block=None):
    channels, height, across = cells.shape
    gathers = block is not None
    turned = cells.transpose(1, 0, 2)
    operands = [turned[:3], turned[height - 3 :]]
    edge = jax.ShapeDtypeStruct((3, channels, across), cells.dtype)
    shapes = [edge, edge]
    scratch = [pltpu.SemaphoreType.DMA((2,)), pltpu.SemaphoreType.DMA((2,))]
    if gathers:
        operands.append(block)
        shapes.append(jax.ShapeDtypeStruct((count,) + block.shape, block.dtype))
        scratch += [
            pltpu.SemaphoreType.DMA((count,)),
            pltpu.SemaphoreType.DMA((count,)),
            pltpu.SemaphoreType.DMA,
        ]
    above, below, *rest = pl.pallas_call(
        functools.partial(halo_kernel, count, gathers),
        out_shape=tuple(shapes),
        in_specs=[VMEM] * len(operands),
        out_specs=(VMEM,) * len(shapes),
        scratch_shapes=scratch,
        compiler_params=pltpu.CompilerParams(collective_id=channel_id, has_side_effects=True),
        name="halo",
    )(*operands)
    me = lax.axis_index("rows")
    above = jnp.where(me > 0, above, jnp.zeros_like(above))
    below = jnp.where(me < count - 1, below, jnp.zeros_like(below))
    spare = jnp.zeros((channels, SLOT - height - 6, across), cells.dtype)
    above, below = above.transpose(1, 0, 2), below.transpose(1, 0, 2)
    return jnp.concatenate([above, cells, below, spare], axis=1), *rest


def sum_kernel(slides, count, part_ref, out_ref, near, half, far, send, recv):
    slide, me = lax.axis_index("slide"), lax.axis_index("rows")
    across = [(lax.rem(slide + k, slides), me) for k in range(1, slides)]
    along = [(slide, lax.rem(me + k, count)) for k in range(1, count)]
    greet(across + along)
    first = [
        remote(part_ref.at[peer[0]], near.at[k], send.at[0, k], recv.at[0, k], peer)
        for k, peer in enumerate(across)
    ]
    for copy in first:
        copy.wait()
    total = part_ref[slide].astype(jnp.float32)
    for k in range(slides - 1):
        total = total + near[k].astype(jnp.float32)
    half[...] = total.astype(jnp.bfloat16)
    second = [
        remote(half.at[peer[1]], far.at[k], send.at[1, k], recv.at[1, k], peer)
        for k, peer in enumerate(along)
    ]
    for copy in second:
        copy.wait()
    total = half[me].astype(jnp.float32)
    for k in range(count - 1):
        total = total + far[k].astype(jnp.float32)
    out_ref[slide, me] = total.astype(jnp.bfloat16)
    third = [
        remote(out_ref.at[slide, me], out_ref.at[slide, me], send.at[2, k], recv.at[2, k], peer)
        for k, peer in enumerate(along)
    ]
    for copy in third:
        copy.wait()
    fourth = [
        remote(out_ref.at[slide], out_ref.at[slide], send.at[3, k], recv.at[3, k], peer)
        for k, peer in enumerate(across)
    ]
    for copy in fourth:
        copy.wait()


def sum_everywhere(rows, slides, count):
    length, across = rows.shape
    share = 16 * pl.cdiv(length, 16 * slides * count)
    padded = jnp.pad(rows, ((0, slides * count * share - length), (0, 0))).astype(jnp.bfloat16)
    shape = (slides, count, share, across)
    totals = pl.pallas_call(
        functools.partial(sum_kernel, slides, count),
        out_shape=jax.ShapeDtypeStruct(shape, jnp.bfloat16),
        in_specs=[VMEM],
        out_specs=VMEM,
        scratch_shapes=[
            pltpu.VMEM((slides - 1,) + shape[1:], jnp.bfloat16),
            pltpu.VMEM(shape[1:], jnp.bfloat16),
            pltpu.VMEM((count - 1,) + shape[2:], jnp.bfloat16),
            pltpu.SemaphoreType.DMA((4, max(slides, count) - 1)),
            pltpu.SemaphoreType.DMA((4, max(slides, count) - 1)),
        ],
        compiler_params=pltpu.CompilerParams(collective_id=2, has_side_effects=True),
        name="sum_everywhere",
    )(padded.reshape(shape))
    return totals.reshape(-1, across)[:length].astype(jnp.float32)


def shifted_stack(rows):
    across = rows.shape[1]
    lane = lax.broadcasted_iota(jnp.int32, rows.shape, 1)
    spare = jnp.zeros((across - PER * SLOT, across), jnp.float32)
    pieces = []
    for b in range(7):
        offset = b - 3
        if offset == 0:
            piece = rows
        else:
            piece = pltpu.roll(rows, (-offset) % across, 1)
            inside = lane < across - offset if offset > 0 else lane >= -offset
            piece = jnp.where(inside, piece, 0.0)
        pieces.append(piece)
        if b % PER == PER - 1:
            pieces.append(spare)
    return jnp.concatenate(pieces, axis=0).astype(jnp.bfloat16)


def banded(taps_ref, c, first, height):
    parts = []
    for g in range(3):
        part = taps_ref[first + g, pl.ds(c, 1), :]
        part = jnp.broadcast_to(part, (height, 128))
        parts.append(pltpu.roll(part, 0, 1, stride=1, stride_axis=0))
    return jnp.concatenate(parts, axis=1)


def diagonal_sums(cells):
    height, across = cells.shape
    total = cells[:8]
    for start in range(8, height, 8):
        total = total + pltpu.roll(cells[start : start + 8], across - start, 1)
    row = lax.broadcasted_iota(jnp.int32, total.shape, 0)
    for bit in (4, 2, 1):
        total = jnp.where((row // bit) % 2 == 1, pltpu.roll(total, across - bit, 1), total)
    return jnp.sum(total, axis=0, keepdims=True)


def forward_kernel(
    ext_ref, taps_ref, channel_ref, up_ref, up_bias, down_ref, mask_ref, branch_ref,
    grad_ref, embed_ref, up_out, down_out, held, sums, hidden_sum, slope_gain,
):
    conv_bias, gain_ref, bias_ref, down_bias = [channel_ref.at[i] for i in range(4)]
    channels, _, across = ext_ref.shape
    height = grad_ref.shape[1]
    hidden_units = up_ref.shape[1]
    depth = 2 * 128 + SLOT

    def conv_channel(c, carry):
        rows = ext_ref[c].astype(jnp.float32)
        stack = shifted_stack(rows)
        hi = banded(taps_ref, c, 0, height)
        lo = banded(taps_ref, channels + c, 0, height)
        left = jnp.concatenate([hi, lo], axis=0).astype(jnp.bfloat16)[:, :depth]
        both = jnp.dot(left, stack, preferred_element_type=jnp.float32)
        held[pl.ds(c, height, stride=channels), :] = both[:height] + both[height:]
        sums[pl.ds(c, 1), :] = jnp.sum(rows, axis=0, keepdims=True) - jnp.sum(
            rows[:3], axis=0, keepdims=True
        ) - jnp.sum(rows[height + 3 :], axis=0, keepdims=True)
        return carry

    lax.fori_loop(0, channels, conv_channel, 0, unroll=8)

    slope_gain[...] = jnp.dot(down_ref[...], branch_ref[...], preferred_element_type=jnp.float32)
    hidden_sum[...] = jnp.zeros_like(hidden_sum)
    up_out[...] = jnp.zeros_like(up_out)

    def pixels(block, carry):
        parts = []
        for r in range(ROWS):
            start = pl.multiple_of((block * ROWS + r) * channels, 8)
            parts.append(held[pl.ds(start, channels), :])
        conv = jnp.concatenate(parts, axis=1) + conv_bias[...]
        average = jnp.mean(conv, axis=0, keepdims=True)
        centered = conv - average
        variance = jnp.mean(centered * centered, axis=0, keepdims=True)
        reciprocal = lax.rsqrt(variance + 1e-06)
        standard = centered * reciprocal
        normed = (standard * gain_ref[...] + bias_ref[...]).astype(jnp.bfloat16)
        act = lax.dot_general(
            up_ref[...], normed, (((0,), (0,)), ((), ())), preferred_element_type=jnp.float32
        )
        act = act + up_bias[...]
        cumulative = 0.5 + 0.5 * lax.erf(act * 0.7071067811865476)
        hidden = (act * cumulative).astype(jnp.bfloat16).astype(jnp.float32)
        total = hidden_sum[...]
        for r in range(ROWS):
            total = total + hidden[:, r * across : (r + 1) * across]
        hidden_sum[...] = total
        density = jnp.exp(-0.5 * act * act) * 0.3989422804014327
        slope = cumulative + act * density
        grad_hidden = jnp.concatenate([slope_gain[...]] * ROWS, axis=1)
        grad_act = (grad_hidden * slope).astype(jnp.bfloat16)
        grad_normed = jnp.dot(up_ref[...], grad_act, preferred_element_type=jnp.float32)
        up_out[...] += lax.dot_general(
            normed, grad_act, (((1,), (1,)), ((), ())), preferred_element_type=jnp.float32
        )
        grad_standard = grad_normed * gain_ref[...]
        first = jnp.mean(grad_standard, axis=0, keepdims=True)
        second = jnp.mean(grad_standard * standard, axis=0, keepdims=True)
        grad_conv = reciprocal * (grad_standard - first - standard * second)
        for r in range(ROWS):
            start = pl.multiple_of((block * ROWS + r) * channels, 8)
            held[pl.ds(start, channels), :] = grad_conv[:, r * across : (r + 1) * across]
        return carry

    lax.fori_loop(0, height // ROWS, pixels, 0)

    total = hidden_sum[...]
    total_hi = total.astype(jnp.bfloat16)
    total_lo = (total - total_hi.astype(jnp.float32)).astype(jnp.bfloat16)
    branch = jnp.zeros((channels, across), jnp.float32)
    down = jnp.zeros((channels, hidden_units), jnp.float32)
    for part in (total_hi, total_lo):
        branch += lax.dot_general(
            down_ref[...], part, (((0,), (0,)), ((), ())), preferred_element_type=jnp.float32
        )
        down += lax.dot_general(
            branch_ref[...], part, (((1,), (1,)), ((), ())), preferred_element_type=jnp.float32
        )
    down_out[...] = down
    embed_ref[...] = sums[...] + mask_ref[...] * (branch + height * down_bias[...])

    def turn(c, carry):
        grad_ref[c] = held[pl.ds(c, height, stride=channels), :].astype(jnp.bfloat16)
        return carry

    lax.fori_loop(0, channels, turn, 0, unroll=8)


def backward_kernel(grad_ref, image_ref, taps_ref, cotangent_ref, out_ref, kernel_ref):
    channels, height, across = image_ref.shape
    depth = 2 * 128 + SLOT

    def channel(c, carry):
        stack = shifted_stack(grad_ref[c].astype(jnp.float32))
        left = banded(taps_ref, c, 3, height).astype(jnp.bfloat16)[:, :depth]
        conv = jnp.dot(left, stack, preferred_element_type=jnp.float32)
        out_ref[c] = (conv + cotangent_ref[pl.ds(c, 1), :]).astype(jnp.bfloat16)
        spare = jnp.zeros((3 * 128 - depth, across), jnp.bfloat16)
        cross = lax.dot_general(
            image_ref[c],
            jnp.concatenate([stack, spare], axis=0),
            (((1,), (1,)), ((), ())),
            preferred_element_type=jnp.float32,
        )
        for g in range(3):
            kernel_ref[g, pl.ds(c, 1), :] = diagonal_sums(cross[:, g * 128 : (g + 1) * 128])
        return carry

    lax.fori_loop(0, channels, channel, 0, unroll=8)


def tap_lanes_of(mirrored):
    places = np.zeros((49, 3 * 128), np.float32)
    for a in range(7):
        for b in range(7):
            tap = 7 * (6 - a) + 6 - b if mirrored else 7 * a + b
            places[tap, 128 * (b // PER) + SLOT * (b % PER) + a] = 1.0
    return places


def taps_of(rows):
    channels = rows.shape[1]
    groups = rows[:, :, : PER * SLOT].transpose(1, 0, 2).reshape(channels, 9, SLOT)
    return groups[:, :7, :7].transpose(0, 2, 1)


def on_device(
    features,
    depth_kernel,
    depth_bias,
    norm_gain,
    norm_bias,
    up_weight,
    up_bias,
    down_weight,
    down_bias,
    layer_scale,
    tissue,
    aggregator_order,
    tile_cotangent,
):
    image = features[0]
    channels, height, across = image.shape
    tiles_here = across // TILE
    hidden_units = up_weight.shape[1]
    taps_hi = lax.reduce_precision(depth_kernel, 8, 7)
    taps_lo = depth_kernel - taps_hi
    both = jnp.concatenate([taps_hi, taps_lo], axis=0).astype(jnp.bfloat16)
    places = np.concatenate([tap_lanes_of(False), tap_lanes_of(True)], axis=1)
    places = places.reshape(49, 6, 128).transpose(1, 0, 2)
    rows = lax.dot_general(
        jnp.broadcast_to(both, (6,) + both.shape),
        jnp.asarray(places, jnp.bfloat16),
        (((2,), (1,)), ((0,), (0,))),
        preferred_element_type=jnp.float32,
    )
    slides, count = lax.axis_size("slide"), lax.axis_size("rows")
    extended, gathered = halo(image, count, 0, tile_cotangent[0])
    gathered = gathered.reshape(count * tiles_here, channels)
    positions = lax.dynamic_slice_in_dim(
        aggregator_order[0], lax.axis_index("rows") * tiles_here, tiles_here
    )
    wanted = jnp.take(gathered, positions, axis=0).astype(jnp.float32)
    cotangent = jnp.repeat(wanted.T, TILE, axis=1)
    mask = jnp.repeat(tissue[0, 0].astype(jnp.float32), TILE)
    scaled_mask = mask[None, :] * layer_scale[:, None]
    grad_branch = (scaled_mask * cotangent).astype(jnp.bfloat16)
    f32 = jnp.float32
    grad_conv, embed, up_term, down_term = pl.pallas_call(
        forward_kernel,
        out_shape=(
            jax.ShapeDtypeStruct((channels, height, across), jnp.bfloat16),
            jax.ShapeDtypeStruct((channels, across), f32),
            jax.ShapeDtypeStruct((channels, hidden_units), f32),
            jax.ShapeDtypeStruct((channels, hidden_units), f32),
        ),
        in_specs=[VMEM] * 8,
        out_specs=(VMEM,) * 4,
        scratch_shapes=[
            pltpu.VMEM((height * channels, across), f32),
            pltpu.VMEM((channels, across), f32),
            pltpu.VMEM((hidden_units, across), f32),
            pltpu.VMEM((hidden_units, across), f32),
        ],
        compiler_params=pltpu.CompilerParams(vmem_limit_bytes=56 * 1024 * 1024),
        name="forward_block",
    )(
        extended,
        rows,
        jnp.stack([depth_bias, norm_gain, norm_bias, down_bias])[:, :, None],
        up_weight,
        up_bias[:, None],
        down_weight,
        scaled_mask,
        grad_branch,
    )
    embedding = (
        embed.reshape(channels, tiles_here, TILE).sum(axis=2) / (height * TILE)
    ).T[None]
    (grad_extended,) = halo(grad_conv, count, 1)
    input_grad, kernel_rows = pl.pallas_call(
        backward_kernel,
        out_shape=(
            jax.ShapeDtypeStruct((channels, height, across), jnp.bfloat16),
            jax.ShapeDtypeStruct((3, channels, 128), f32),
        ),
        in_specs=[VMEM] * 4,
        out_specs=(VMEM,) * 2,
        compiler_params=pltpu.CompilerParams(vmem_limit_bytes=40 * 1024 * 1024),
        name="backward_conv",
    )(grad_extended, image, rows, cotangent)
    kernel_term = taps_of(kernel_rows)[:, ::-1, ::-1].reshape(channels, 49)
    loss_norm = 1.0 / math.sqrt(slides * count * height * across)
    tap_lanes = kernel_term.shape[1]
    wide = jnp.pad(kernel_term, ((0, 0), (0, across - tap_lanes)))
    blocks = hidden_units // across
    combined = jnp.concatenate(
        [
            up_term.reshape(channels, blocks, across).transpose(1, 0, 2),
            down_term.reshape(channels, blocks, across).transpose(1, 0, 2),
            wide[None],
        ],
        axis=0,
    )
    totals = sum_everywhere((combined * loss_norm).reshape(-1, across), slides, count)
    totals = totals.reshape(2 * blocks + 1, channels, across)
    grad_up = totals[:blocks].transpose(1, 0, 2).reshape(channels, hidden_units)
    grad_down = totals[blocks : 2 * blocks].transpose(0, 2, 1).reshape(hidden_units, channels)
    grad_kernel = totals[2 * blocks, :, :tap_lanes]
    return (embedding, input_grad[None], grad_up, grad_down, grad_kernel)


def solution(mesh):
    return jax.shard_map(
        on_device,
        mesh=mesh,
        in_specs=(
            P("slide", None, "rows", None),
            P(),
            P(),
            P(),
            P(),
            P(),
            P(),
            P(),
            P(),
            P(),
            P("slide", "rows", None),
            P("slide", None),
            P("slide", "rows", None),
        ),
        out_specs=(P("slide", "rows", None), P("slide", None, "rows", None), P(), P(), P()),
        check_vma=False,
    )
```

profile of v0, /device:TPU:1, one launch (start us, length us, event | category | flops | bytes accessed | tf_op | source)
XLA Modules:
  0.0 142.9 jit_solution(16634080024123513208)
XLA Ops:
  0.6 0.0 copy-start.1
  0.7 0.8 convert_bitcast_fusion.1
  1.4 0.7 fusion.8
  2.2 0.7 compare_and_fusion
  2.9 0.1 pad.27.clone
  3.0 0.1 broadcast_in_dim.38
  3.0 0.1 mul.31
  3.1 0.7 maximum_bitcast_fusion
  3.9 0.8 reduce-precision_convert_fusion
  4.7 0.1 pad_maximum_fusion
  4.8 1.0 copy.75.channel_ref
  5.7 0.0 copy-start.6
  5.7 1.6 %broadcast_in_dim.45.up_bias = f32[768,1]{1,0:T(8,128)} reshape(f32[768]{0:T(1024)} %param.20) | data formatting | bytes 6144 | tf_op jit(solution)/shard_map/broadcast_in_dim | solution.py:400
  7.4 0.0 copy-start.5
  7.4 1.9 %copy.77.down_ref = bf16[768,192]{1,0:T(8,128)(2,1)} copy(bf16[768,192]{0,1:T(8,128)(2,1)} %param.21) | data formatting | bytes 589824 | tf_op args[7]
  9.3 0.0 copy-done.1
  9.3 0.2 fusion.10
  9.5 0.7 copy.71.tail_ref
  10.1 0.7 copy.70.head_ref
  10.8 13.9 %halo.2 = (bf16[3,192,128]{2,1,0:T(8,128)(2,1)}, bf16[3,192,128]{2,1,0:T(8,128)(2,1)}, bf16[8,4,192]{2,1,0:T(4,128)(2,1)}) custom-call(bf16[3,192,128]{2,1,0:T(8,128)(2,1)} %copy.70.head_ref, bf16[3,192,128]{2,1,0:T(8,128)(2,1)} %copy.71.tail_ref, bf16[4,192]{1,0:T(4,128)(2,1)} %bitcast.99), custom_call_target="tpu_custom_call" | custom-call | tf_op jit(solution)/shard_map/halo/pallas_call | solution.py:87
  24.7 0.7 reshape.91
  25.5 0.6 gather_fusion
  26.0 0.1 convert_bitcast_fusion
  26.1 1.3 fusion.3
  27.4 0.1 copy.74.cotangent_ref
  27.5 0.0 copy-done.6
  27.5 0.7 multiply_convert_fusion
  28.3 0.0 copy-done.5
  28.3 1.4 fusion.5.taps_ref
  29.7 2.5 %maximum_maximum_fusion.ext_ref = bf16[192,40,128]{2,1,0:T(8,128)(2,1)} fusion(bf16[192,3,128]{2,1,0:T(4,128)(2,1)S(1)} %get-tuple-element.52, bf16[192,32,128]{2,1,0:T(8,128)(2,1)S(1)} %bitcast.84, bf16[192,3,128]{2,1,0:T(4,128)(2,1)S(1)} %get-tuple-element.53, bf16[40]{0:T(256)(128)(2,1)S(1)} %pad.27.clone), kind=kLoop, calls=%fused_computation.1 | loop fusion | flops 7864320 | bytes 3833936 | tf_op jit(solution)/shard_map/concatenate | solution.py:101
  32.1 30.9 %forward_block.1 = (bf16[192,32,128]{2,1,0:T(8,128)(2,1)}, f32[192,128]{1,0:T(8,128)}, f32[192,768]{1,0:T(8,128)}, f32[192,768]{1,0:T(8,128)}) custom-call(bf16[192,40,128]{2,1,0:T(8,128)(2,1)} %maximum_maximum_fusion.ext_ref, f32[6,384,128]{2,1,0:T(8,128)} %fusion.5.taps_ref, f32[4,192,1]{2,1,0:T(8,128)} %copy.75.channel_ref, bf16[192,768]{1,0:T(8,128)(2,1)} %up_ref.1, ...), custom_call_target="tpu_custom_call" | custom-call | tf_op jit(solution)/shard_map/forward_block/pallas_call | solution.py:377
  63.1 0.0 copy-start.2
  63.1 1.1 copy.78
  64.2 0.6 multiply_bitcast_fusion
  64.8 1.9 %bitcast_bitcast_fusion.1 = f32[6,192,128]{2,1,0:T(8,128)} fusion(f32[192,768]{1,0:T(8,128)} %get-tuple-element.24), kind=kLoop, calls=%fused_computation.10 | loop fusion | bytes 1179648 | tf_op jit(solution)/shard_map/transpose | solution.py:427
  66.7 1.9 %bitcast_bitcast_fusion = f32[6,192,128]{2,1,0:T(8,128)} fusion(f32[192,768]{1,0:T(8,128)} %get-tuple-element.25), kind=kLoop, calls=%fused_computation.9 | loop fusion | bytes 1179648 | tf_op jit(solution)/shard_map/transpose | solution.py:428
  68.6 0.0 copy-done.2
  68.6 0.6 copy.112
  69.3 0.7 fusion.9
  70.0 9.8 %halo.3 = (bf16[3,192,128]{2,1,0:T(8,128)(2,1)}, bf16[3,192,128]{2,1,0:T(8,128)(2,1)}) custom-call(bf16[3,192,128]{2,1,0:T(8,128)(2,1)} %get-tuple-element.43.head_ref, bf16[3,192,128]{2,1,0:T(8,128)(2,1)} %get-tuple-element.42.tail_ref), custom_call_target="tpu_custom_call" | custom-call | tf_op jit(solution)/shard_map/halo/pallas_call | solution.py:87
  79.8 1.1 fusion.2
  80.8 1.1 fusion.1
  81.9 0.0 copy-start
  81.9 1.2 maximum_maximum_fusion.1.grad_ref
  83.1 0.1 copy-done
  83.2 19.9 %backward_conv.1 = (bf16[192,32,128]{2,1,0:T(8,128)(2,1)}, f32[3,192,128]{2,1,0:T(8,128)S(1)}) custom-call(bf16[192,40,128]{2,1,0:T(8,128)(2,1)S(1)} %maximum_maximum_fusion.1.grad_ref, bf16[192,32,128]{2,1,0:T(8,128)(2,1)S(1)} %bitcast.85, f32[6,384,128]{2,1,0:T(8,128)S(1)} %copy-done, f32[192,128]{1,0:T(8,128)S(1)} %copy.74.cotangent_ref), custom_call_target="tpu_custom_call" | custom-call | tf_op jit(solution)/shard_map/backward_conv/pallas_call | solution.py:409
  103.0 0.0 copy-start.3
  103.0 0.0 copy-start.4
  103.1 0.2 copy.85
  103.2 0.1 rev.3
  103.4 0.1 copy.87
  103.5 0.6 copy-done.3
  104.1 0.2 copy-done.4
  104.3 0.2 fusion
  104.4 0.9 pad.10
  105.3 33.0 %sum_everywhere.1 = bf16[4,8,80,128]{3,2,1,0:T(8,128)(2,1)} custom-call(bf16[4,8,80,128]{3,2,1,0:T(8,128)(2,1)} %bitcast.89), custom_call_target="tpu_custom_call" | custom-call | tf_op jit(solution)/shard_map/sum_everywhere/pallas_call | solution.py:148
  138.3 1.2 slice_convert_fusion
  139.5 0.7 copy.90
  140.2 0.1 fusion.11
  140.3 0.4 copy.88
  140.7 0.9 copy.114
  141.6 0.4 copy.89
  142.0 0.9 copy.113
  (10 shorter events, 0.1 us)
Async XLA Ops:
  0.6 8.7 %copy-start.1 = (bf16[1,192,32,128]{3,2,1,0:T(8,128)(2,1)S(1)}, bf16[1,192,32,128]{3,2,1,0:T(8,128)(2,1)}, u32[]{:S(2)}) copy-start(bf16[1,192,32,128]{3,2,1,0:T(8,128)(2,1)} %param.14) | copy-start | bytes 4718596
  5.7 21.8 %copy-start.6 = (f32[192]{0:T(256)S(1)}, f32[192]{0:T(256)}, u32[]{:S(2)}) copy-start(f32[192]{0:T(256)} %param.23) | copy-start | bytes 2308
  7.4 20.9 %copy-start.5 = (bf16[6,49,128]{2,1,0:T(8,128)(2,1)S(1)}, bf16[6,49,128]{2,1,0:T(8,128)(2,1)}, u32[]{:S(2)}) copy-start(bf16[6,49,128]{2,1,0:T(8,128)(2,1)} %constant.41.clone) | copy-start | bytes 225796
  63.1 5.6 %copy-start.2 = (bf16[192,32,128]{2,1,0:T(8,128)(2,1)S(1)}, bf16[192,32,128]{2,1,0:T(8,128)(2,1)}, u32[]{:S(2)}) copy-start(bf16[192,32,128]{2,1,0:T(8,128)(2,1)} %get-tuple-element.20) | copy-start | bytes 4718596
  81.9 1.3 copy-start
  103.0 1.1 copy-start.3
  103.0 1.2 copy-start.4
where the time goes:
time: 144 us; the launch traced here: 143 us
  Pallas kernels  107 us (74%)
  local copies, waits for them, and re-layouts  19.5 us (14%)
  other arithmetic  13.7 us (10%)
    pallas_call x1, Pallas kernels, sum_everywhere(): pl.pallas_call(functools.partial(sum_kernel, slides, count), out_shape=ja...  33 us
    pallas_call x1, Pallas kernels, on_device(): pl.pallas_call(forward_kernel, out_shape=(jax.ShapeDtypeStruct((channels,...  30.9 us
    pallas_call x2, Pallas kernels, halo(): pl.pallas_call(functools.partial(halo_kernel, count, gathers), out_shape=...  23.7 us
    pallas_call x1, Pallas kernels, on_device(): pl.pallas_call(backward_kernel, out_shape=(jax.ShapeDtypeStruct((channels...  19.9 us
    unnamed x18, local copies, waits for them, and re-layouts  5.37 us
    concatenate x2, other arithmetic, halo(): return (jnp.concatenate([above, cells, below, spare], axis=1), *rest)  3.64 us
    transpose x3, other arithmetic, halo(): above, below = (above.transpose(1, 0, 2), below.transpose(1, 0, 2))  3.36 us

commit v1 on v0

v1 whole, which is shorter than its diff:
```python
import functools
import math

import jax
import jax.numpy as jnp
from jax import lax
from jax.experimental import pallas as pl
from jax.experimental.pallas import tpu as pltpu
from jax.sharding import PartitionSpec as P

TILE = 32
ROWS = 4
HALF = 16
TAPS = 7
PAD = 3
EDGE = 4
LANES = 128
MESH = pl.DeviceIdType.MESH
VMEM = pl.BlockSpec(memory_space=pltpu.VMEM)
SMEM = pl.BlockSpec(memory_space=pltpu.SMEM)
F32 = jnp.float32
BF16 = jnp.bfloat16


def remote(source, target, send, receive, peer):
    return pltpu.make_async_remote_copy(
        src_ref=source,
        dst_ref=target,
        send_sem=send,
        recv_sem=receive,
        device_id=peer,
        device_id_type=MESH,
    )


def dot(left, right, contract):
    return lax.dot_general(left, right, ((contract[:1], contract[1:]), ((), ())), preferred_element_type=F32)


def split(values, parts):
    pieces = []
    for _ in range(parts):
        piece = values.astype(BF16)
        pieces.append(piece)
        values = values - piece.astype(F32)
    return pieces


def place_taps(hi_lo, b, mirrored, hi_at, lo_at):
    rows = hi_lo.shape[0]
    count = TAPS * TAPS
    row = lax.broadcasted_iota(jnp.int32, (rows, LANES), 0)
    lane = lax.broadcasted_iota(jnp.int32, (rows, LANES), 1)
    low = row >= count
    tap = jnp.where(low, row - count, row)
    a, column = lax.div(tap, TAPS), lax.rem(tap, TAPS)
    if mirrored:
        a, column = TAPS - 1 - a, TAPS - 1 - column
    at = jnp.where(low, lo_at, hi_at) + a
    places = jnp.where((column == b) & (lane == at), 1.0, 0.0).astype(BF16)
    return dot(hi_lo, places, (0, 0))


def banded(taps_ref, c, depth):
    parts = []
    for b in range(TAPS):
        part = jnp.broadcast_to(taps_ref[b, pl.ds(c, 1), :], (HALF, LANES))
        parts.append(pltpu.roll(part, 0, 1, stride=1, stride_axis=0))
    return jnp.concatenate(parts, axis=0).astype(BF16)[:, :depth]


def gather_columns(stacked, across):
    lane = lax.broadcasted_iota(jnp.int32, (2 * HALF, across), 1)

    def part(b):
        rows = stacked[b * HALF : (b + 1) * HALF]
        return jnp.concatenate([rows[:, :across], rows[:, across:]], axis=0)

    def leftward(cells):
        return jnp.where(lane < across - 1, pltpu.roll(cells, across - 1, 1), 0.0)

    def rightward(cells):
        return jnp.where(lane > 0, pltpu.roll(cells, 1, 1), 0.0)

    left = part(4) + leftward(part(5) + leftward(part(6)))
    right = part(2) + rightward(part(1) + rightward(part(0)))
    return part(3) + leftward(left) + rightward(right)


def windows(image_ref, halo_ref, c):
    image = image_ref[0, c]
    spare = jnp.zeros((HALF - EDGE, image.shape[1]), F32)
    above = jnp.concatenate([spare, halo_ref[0, c].astype(F32)], axis=0).astype(BF16)
    below = jnp.concatenate([halo_ref[1, c].astype(F32), spare], axis=0).astype(BF16)
    top, bottom = image[:HALF], image[HALF:]
    return [
        jnp.concatenate(pair, axis=1) for pair in ((above, top), (top, bottom), (bottom, below))
    ]


def block_kernel(
    slides, count, share, order_ref, tissue_ref, image_ref, tile_ref, taps_in, channel_ref,
    up_ref, up_bias_ref, down_ref,
    embed_out, grad_out, up_out, down_out, kernel_out,
    fore_taps, back_taps, halo_out, halo_in, tiles_in, held, sums, hidden_sum, slope_gain,
    up_total, cotangent, scaled_mask, columns, bias, edge_out, edge_in, crossed,
    part, near, half, far, whole_sum, kpart, knear, khalf, kfar, kwhole,
    halo_sem, tile_sem, edge_sem, sum_sem, ksum_sem,
):
    slide, me = lax.axis_index("slide"), lax.axis_index("rows")
    channels, height, across = image_ref.shape[1:]
    hidden_units = up_ref.shape[1]
    tiles_here = across // TILE
    across_peers = [(lax.rem(slide + k, slides), me) for k in range(1, slides)]
    along_peers = [(slide, lax.rem(me + k, count)) for k in range(1, count)]
    up_peer, down_peer = along_peers[-1], along_peers[0]
    has_up, has_down = me > 0, me < count - 1

    def edges(out, into, sem):
        return (
            remote(out.at[0], into.at[0], sem.at[0], sem.at[2], down_peer),
            remote(out.at[1], into.at[1], sem.at[1], sem.at[3], up_peer),
        )

    def start_edges(pair):
        pl.when(has_down)(pair[0].start)
        pl.when(has_up)(pair[1].start)

    def finish_edges(pair):
        pl.when(has_down)(pair[0].wait_send)
        pl.when(has_up)(pair[1].wait_send)
        pl.when(has_up)(pair[0].wait_recv)
        pl.when(has_down)(pair[1].wait_recv)

    def pack_edges(c, carry):
        halo_out[0, c] = image_ref[0, c, height - EDGE :, :]
        halo_out[1, c] = image_ref[0, c, :EDGE, :]
        return carry

    barrier = pltpu.get_barrier_semaphore()
    for peer in across_peers + along_peers:
        pl.semaphore_signal(barrier, inc=1, device_id=peer, device_id_type=MESH)
    lax.fori_loop(0, channels, pack_edges, 0, unroll=8)

    @pl.when(jnp.logical_not(has_up))
    def _():
        halo_in[0] = jnp.zeros(halo_in.shape[1:], BF16)
        edge_in[0] = jnp.zeros(edge_in.shape[1:], BF16)

    @pl.when(jnp.logical_not(has_down))
    def _():
        halo_in[1] = jnp.zeros(halo_in.shape[1:], BF16)
        edge_in[1] = jnp.zeros(edge_in.shape[1:], BF16)

    pl.semaphore_wait(barrier, slides + count - 2)
    halo_copies = edges(halo_out, halo_in, halo_sem)
    start_edges(halo_copies)
    tile_copies = [
        remote(tile_ref.at[0], tiles_in.at[me], tile_sem.at[0, k], tile_sem.at[1, k], peer)
        for k, peer in enumerate(along_peers)
    ]
    for copy in tile_copies:
        copy.start()
    tiles_in[me] = tile_ref[0]

    hi_lo = jnp.concatenate([p.astype(F32) for p in split(taps_in[...], 2)], axis=0).astype(BF16)
    for b in range(TAPS):
        fore_taps[b] = place_taps(hi_lo, b, False, HALF - PAD, 4 * HALF - PAD)
        back_taps[b] = place_taps(hi_lo, b, True, 0, HALF + 8)

    turned = jnp.transpose(channel_ref[...])
    for k in range(columns.shape[0]):
        columns[k] = jnp.broadcast_to(turned[:, k : k + 1], (channels, across))
    turned = jnp.transpose(up_bias_ref[...])
    for k in range(hidden_units // LANES):
        bias[k * LANES : (k + 1) * LANES] = jnp.broadcast_to(turned[:, k : k + 1], (LANES, across))
    conv_bias, gain, norm_bias, down_bias, scale = [columns.at[k] for k in range(5)]
    lane = lax.broadcasted_iota(jnp.int32, (1, across), 1)
    mask = jnp.zeros((1, across), F32)
    wanted = jnp.zeros((1, across), jnp.int32)
    for t in range(tiles_here):
        here = lax.div(lane, TILE) == t
        mask = jnp.where(here, tissue_ref[0, 0, t].astype(F32), mask)
        wanted = jnp.where(here, order_ref[0, me * tiles_here + t], wanted)
    scaled_mask[...] = scale[...] * mask
    up_total[...] = jnp.zeros_like(up_total)
    hidden_sum[...] = jnp.zeros_like(hidden_sum)
    held[(height + 2 * PAD) * channels :, :] = jnp.zeros((2 * channels, across), F32)

    for copy in tile_copies:
        copy.wait()
    tiles = jnp.concatenate([tiles_in[k].astype(F32) for k in range(count)], axis=0).astype(BF16)
    chosen = lax.broadcasted_iota(jnp.int32, (tiles.shape[0], across), 0) == wanted
    cotangent[...] = dot(tiles, jnp.where(chosen, 1.0, 0.0).astype(BF16), (0, 0))
    grad_branch = (scaled_mask[...] * cotangent[...]).astype(BF16)
    slope_gain[...] = dot(down_ref[...], grad_branch, (0, 0))

    finish_edges(halo_copies)

    fore_depth = 6 * HALF
    ones = jnp.where(
        (lax.broadcasted_iota(jnp.int32, (HALF, fore_depth), 1) >= HALF)
        & (lax.broadcasted_iota(jnp.int32, (HALF, fore_depth), 1) < 3 * HALF),
        1.0,
        0.0,
    ).astype(BF16)

    def conv_channel(c, carry):
        pieces = windows(image_ref, halo_in, c)
        left = jnp.concatenate([banded(fore_taps, c, fore_depth), ones], axis=0)
        stacked = dot(left, jnp.concatenate(pieces + pieces, axis=0), (1, 0))
        held[pl.ds(PAD * channels + c, height, stride=channels), :] = gather_columns(stacked, across)
        sums[pl.ds(c, 1), :] = stacked[TAPS * HALF : TAPS * HALF + 1, :across]
        return carry

    lax.fori_loop(0, channels, conv_channel, 0, unroll=8)

    blocks = height // ROWS
    edge_copies = edges(edge_out, edge_in, edge_sem)

    def pixels(step, carry):
        block = jnp.where(step == 0, 0, jnp.where(step == 1, blocks - 1, step - 1))

        def start_of(r):
            return pl.multiple_of((block * ROWS + r + PAD) * channels, 8)

        def wide(ref):
            return jnp.concatenate([ref[...]] * ROWS, axis=1)

        conv = jnp.concatenate([held[pl.ds(start_of(r), channels), :] for r in range(ROWS)], axis=1)
        conv = conv + wide(conv_bias)
        average = jnp.mean(conv, axis=0, keepdims=True)
        centered = conv - average
        variance = jnp.mean(centered * centered, axis=0, keepdims=True)
        reciprocal = lax.rsqrt(variance + 1e-06)
        standard = centered * reciprocal
        normed = (standard * wide(gain) + wide(norm_bias)).astype(BF16)
        act = dot(up_ref[...], normed, (0, 0)) + wide(bias)
        cumulative = 0.5 + 0.5 * lax.erf(act * 0.7071067811865476)
        hidden = (act * cumulative).astype(BF16).astype(F32)
        total = hidden_sum[...]
        for r in range(ROWS):
            total = total + hidden[:, r * across : (r + 1) * across]
        hidden_sum[...] = total
        density = jnp.exp(-0.5 * act * act) * 0.3989422804014327
        slope = cumulative + act * density
        grad_act = (wide(slope_gain) * slope).astype(BF16)
        grad_normed = dot(up_ref[...], grad_act, (1, 0))
        up_total[...] += dot(normed, grad_act, (1, 1))
        grad_standard = grad_normed * wide(gain)
        first = jnp.mean(grad_standard, axis=0, keepdims=True)
        second = jnp.mean(grad_standard * standard, axis=0, keepdims=True)
        grad_conv = reciprocal * (grad_standard - first - standard * second)
        for r in range(ROWS):
            held[pl.ds(start_of(r), channels), :] = grad_conv[:, r * across : (r + 1) * across]

        @pl.when(step == 1)
        def _():
            for r in range(PAD):
                low = (height + r) * channels
                edge_out[0, r] = held[low : low + channels, :].astype(BF16)
                low = (PAD + r) * channels
                edge_out[1, r] = held[low : low + channels, :].astype(BF16)
            start_edges(edge_copies)

        return carry

    lax.fori_loop(0, blocks, pixels, 0)

    loss_norm = 1.0 / math.sqrt(slides * count * height * across)
    total_parts = split(hidden_sum[...], 2)
    branch = jnp.zeros((channels, across), F32)
    down = jnp.zeros((channels, hidden_units), F32)
    grad_branch = (scaled_mask[...] * cotangent[...]).astype(BF16)
    for piece in total_parts:
        branch += dot(down_ref[...], piece, (1, 0))
        down += dot(grad_branch, piece, (1, 1))
    embed = sums[...] + scaled_mask[...] * (branch + height * down_bias[...])
    tile_of = lax.div(lax.broadcasted_iota(jnp.int32, (tiles_here, across), 1), TILE)
    picks = jnp.where(
        tile_of == lax.broadcasted_iota(jnp.int32, (tiles_here, across), 0), 1.0, 0.0
    ).astype(BF16)
    embedded = jnp.zeros((tiles_here, channels), F32)
    for piece in split(embed, 3):
        embedded += dot(picks, piece, (1, 1))
    embed_out[0] = embedded * (1.0 / (height * TILE))

    groups = hidden_units // LANES
    pieces = channels // HALF

    def slot_of(index):
        shard, offset = divmod(index * HALF, share)
        return shard // count, shard % count, offset

    used = 2 * groups * pieces
    for index in range(slides * count * share // HALF):
        s, r, offset = slot_of(index)
        if index >= used:
            part[s, r, offset : offset + HALF, :] = jnp.zeros((HALF, LANES), BF16)
            continue
        group, piece = divmod(index, pieces)
        low = piece * HALF
        if group < groups:
            values = up_total[low : low + HALF, group * LANES : (group + 1) * LANES]
        else:
            at = (group - groups) * LANES
            values = down[low : low + HALF, at : at + LANES]
        part[s, r, offset : offset + HALF, :] = (values * loss_norm).astype(BF16)

    def sum_slides(part_ref, near_ref, sem):
        return [
            remote(part_ref.at[peer[0]], near_ref.at[k], sem.at[0, k], sem.at[1, k], peer)
            for k, peer in enumerate(across_peers)
        ]

    def sum_rows(half_ref, far_ref, sem):
        return [
            remote(half_ref.at[peer[1]], far_ref.at[k], sem.at[2, k], sem.at[3, k], peer)
            for k, peer in enumerate(along_peers)
        ]

    def start(copies):
        for copy in copies:
            copy.start()

    def finish(copies):
        for copy in copies:
            copy.wait()

    first = sum_slides(part, near, sum_sem)
    start(first)

    band_row = lax.broadcasted_iota(jnp.int32, (2 * HALF, LANES), 0) + 8
    band_lane = lax.broadcasted_iota(jnp.int32, (2 * HALF, LANES), 1)
    tap = band_row - (HALF - PAD) - lax.rem(band_lane, HALF)
    in_band = (tap >= 0) & (tap < TAPS) & (band_lane < TAPS * HALF)
    fold_row = lax.broadcasted_iota(jnp.int32, (8, LANES), 0)
    row_lane = lax.broadcasted_iota(jnp.int32, (height, across), 1)

    def cross_channel(c, carry):
        grad = held[pl.ds(PAD * channels + c, height, stride=channels), :].astype(BF16)
        rows = []
        for b in range(TAPS):
            s = b - PAD
            moved = grad
            if s:
                moved = pltpu.roll(grad, s % across, 1)
                inside = row_lane >= s if s > 0 else row_lane < across + s
                moved = jnp.where(inside, moved, jnp.zeros((), BF16))
            rows.append(jnp.concatenate([moved[:HALF], moved[HALF:]], axis=1))
        rows.append(jnp.zeros((HALF, 2 * across), BF16))
        image = jnp.concatenate(windows(image_ref, halo_in, c), axis=0)
        cross = dot(image, jnp.concatenate(rows, axis=0), (1, 1))[8 : 8 + 2 * HALF]
        cross = jnp.where(in_band, cross, 0.0)
        total = cross[:8]
        for low in range(8, 2 * HALF, 8):
            total = total + pltpu.roll(cross[low : low + 8], LANES - low, 1)
        for bit in (4, 2, 1):
            moves = lax.rem(lax.div(fold_row, bit), 2) == 1
            total = jnp.where(moves, pltpu.roll(total, LANES - bit, 1), total)
        crossed[pl.ds(pl.multiple_of(c * 8, 8), 8), :] = total
        return carry

    lax.fori_loop(0, channels, cross_channel, 0, unroll=8)

    kernel_term = crossed[pl.ds(0, channels, stride=8), :]
    for k in range(1, 8):
        kernel_term = kernel_term + crossed[pl.ds(k, channels, stride=8), :]
    kernel_term = kernel_term * loss_norm
    kpart[...] = jnp.zeros_like(kpart)
    step_rows = channels // count
    for k in range(count):
        low = k * step_rows
        kpart[k, :step_rows, :] = kernel_term[low : low + step_rows].astype(BF16)
    kfirst = [
        remote(kpart, knear.at[k], ksum_sem.at[0, k], ksum_sem.at[1, k], peer)
        for k, peer in enumerate(across_peers)
    ]
    start(kfirst)

    finish(first)
    for r in range(count):
        total = part[slide, r].astype(F32)
        for k in range(slides - 1):
            total = total + near[k, r].astype(F32)
        half[r] = total.astype(BF16)
    second = sum_rows(half, far, sum_sem)
    start(second)

    finish_edges(edge_copies)
    for r in range(PAD):
        held[r * channels : (r + 1) * channels, :] = edge_in[0, r].astype(F32)
        low = (PAD + height + r) * channels
        held[low : low + channels, :] = edge_in[1, r].astype(F32)

    def back_channel(c, carry):
        grad = held[pl.ds(c, height + 8, stride=channels), :]
        pair = jnp.concatenate([grad[: HALF + 8], grad[HALF:]], axis=1)
        right = jnp.concatenate([pair, pair], axis=0).astype(BF16)
        stacked = dot(banded(back_taps, c, right.shape[0]), right, (1, 0))
        conv = gather_columns(stacked, across)
        grad_out[0, c] = (conv + cotangent[pl.ds(c, 1), :]).astype(BF16)
        return carry

    third_of = channels // 3
    lax.fori_loop(0, third_of, back_channel, 0, unroll=8)

    finish(kfirst)
    for r in range(count):
        total = kpart[r].astype(F32)
        for k in range(slides - 1):
            total = total + knear[k, r].astype(F32)
        khalf[r] = total.astype(BF16)
    ksecond = sum_rows(khalf, kfar, ksum_sem)
    start(ksecond)
    finish(second)
    total = half[me].astype(F32)
    for k in range(count - 1):
        total = total + far[k].astype(F32)
    whole_sum[slide, me] = total.astype(BF16)
    third = [
        remote(whole_sum.at[slide, me], whole_sum.at[slide, me], sum_sem.at[4, k], sum_sem.at[5, k], peer)
        for k, peer in enumerate(along_peers)
    ]
    start(third)

    lax.fori_loop(third_of, 2 * third_of, back_channel, 0, unroll=8)

    finish(ksecond)
    total = khalf[me].astype(F32)
    for k in range(count - 1):
        total = total + kfar[k].astype(F32)
    kwhole[me] = total.astype(BF16)
    kthird = [
        remote(kwhole.at[me], kwhole.at[me], ksum_sem.at[4, k], ksum_sem.at[5, k], peer)
        for k, peer in enumerate(along_peers)
    ]
    start(kthird)
    finish(third)
    fourth = [
        remote(whole_sum.at[slide], whole_sum.at[slide], sum_sem.at[6, k], sum_sem.at[7, k], peer)
        for k, peer in enumerate(across_peers)
    ]
    start(fourth)

    lax.fori_loop(2 * third_of, channels, back_channel, 0, unroll=8)

    finish(kthird)
    rows = jnp.concatenate([kwhole[k, :step_rows, :].astype(F32) for k in range(count)], axis=0)
    tap = lax.broadcasted_iota(jnp.int32, (TAPS * TAPS, LANES), 0)
    at = HALF * lax.rem(tap, TAPS) - lax.div(tap, TAPS) - (HALF - PAD) + 8 + LANES
    at = lax.rem(at, LANES) == lax.broadcasted_iota(jnp.int32, (TAPS * TAPS, LANES), 1)
    kernel_out[...] = dot(jnp.where(at, 1.0, 0.0).astype(BF16), rows.astype(BF16), (1, 1))
    finish(fourth)
    for index in range(used):
        s, r, offset = slot_of(index)
        group, piece = divmod(index, pieces)
        low = piece * HALF
        values = whole_sum[s, r, offset : offset + HALF, :].astype(F32)
        target = up_out if group < groups else down_out
        at = group % groups * LANES
        target[low : low + HALF, at : at + LANES] = values


def on_device(
    features,
    depth_kernel,
    depth_bias,
    norm_gain,
    norm_bias,
    up_weight,
    up_bias,
    down_weight,
    down_bias,
    layer_scale,
    tissue,
    aggregator_order,
    tile_cotangent,
):
    channels, height, across = features.shape[1:]
    hidden_units = up_weight.shape[1]
    tiles_here = across // TILE
    slides, count = lax.axis_size("slide"), lax.axis_size("rows")
    entries = 2 * channels * hidden_units // LANES
    share = HALF * pl.cdiv(entries, HALF * slides * count)
    kshare = HALF * pl.cdiv(channels // count, HALF)
    span = (slides, count, share, LANES)
    kspan = (count, kshare, LANES)
    most = max(slides, count) - 1
    dma = pltpu.SemaphoreType.DMA
    embedding, input_grad, grad_up, grad_down, grad_kernel = pl.pallas_call(
        functools.partial(block_kernel, slides, count, share),
        out_shape=(
            jax.ShapeDtypeStruct((1, tiles_here, channels), F32),
            jax.ShapeDtypeStruct(features.shape, BF16),
            jax.ShapeDtypeStruct((channels, hidden_units), F32),
            jax.ShapeDtypeStruct((channels, hidden_units), F32),
            jax.ShapeDtypeStruct((TAPS * TAPS, channels), F32),
        ),
        in_specs=[SMEM, SMEM] + [VMEM] * 7,
        out_specs=(VMEM,) * 5,
        scratch_shapes=[
            pltpu.VMEM((TAPS, channels, LANES), F32),
            pltpu.VMEM((TAPS, channels, LANES), F32),
            pltpu.VMEM((2, channels, EDGE, across), BF16),
            pltpu.VMEM((2, channels, EDGE, across), BF16),
            pltpu.VMEM((count, tiles_here, channels), BF16),
            pltpu.VMEM(((height + 8) * channels, across), F32),
            pltpu.VMEM((channels, across), F32),
            pltpu.VMEM((hidden_units, across), F32),
            pltpu.VMEM((hidden_units, across), F32),
            pltpu.VMEM((channels, hidden_units), F32),
            pltpu.VMEM((channels, across), F32),
            pltpu.VMEM((channels, across), F32),
            pltpu.VMEM((5, channels, across), F32),
            pltpu.VMEM((hidden_units, across), F32),
            pltpu.VMEM((2, PAD, channels, across), BF16),
            pltpu.VMEM((2, PAD, channels, across), BF16),
            pltpu.VMEM((channels * 8, LANES), F32),
            pltpu.VMEM(span, BF16),
            pltpu.VMEM((slides - 1,) + span[1:], BF16),
            pltpu.VMEM(span[1:], BF16),
            pltpu.VMEM((count - 1,) + span[2:], BF16),
            pltpu.VMEM(span, BF16),
            pltpu.VMEM(kspan, BF16),
            pltpu.VMEM((slides - 1,) + kspan, BF16),
            pltpu.VMEM(kspan, BF16),
            pltpu.VMEM((count - 1,) + kspan[1:], BF16),
            pltpu.VMEM(kspan, BF16),
            dma((4,)),
            dma((2, most)),
            dma((4,)),
            dma((8, most)),
            dma((6, most)),
        ],
        compiler_params=pltpu.CompilerParams(
            collective_id=0, has_side_effects=True, vmem_limit_bytes=56 * 1024 * 1024
        ),
        name="block",
    )(
        aggregator_order,
        tissue,
        features,
        tile_cotangent,
        depth_kernel.T,
        jnp.stack([depth_bias, norm_gain, norm_bias, down_bias, layer_scale] + [layer_scale] * 3),
        up_weight,
        up_bias.reshape(-1, LANES),
        down_weight.T,
    )
    return embedding, input_grad, grad_up, grad_down.T, grad_kernel.T


def solution(mesh):
    return jax.shard_map(
        on_device,
        mesh=mesh,
        in_specs=(
            P("slide", None, "rows", None),
            P(),
            P(),
            P(),
            P(),
            P(),
            P(),
            P(),
            P(),
            P(),
            P("slide", "rows", None),
            P("slide", None),
            P("slide", "rows", None),
        ),
        out_specs=(P("slide", "rows", None), P("slide", None, "rows", None), P(), P(), P()),
        check_vma=False,
    )
```

time: 144 us -> 89.5 us (0.62)
  Pallas kernels: 107 us -> 80.5 us
  other arithmetic: 13.7 us -> 0 us
  local copies, waits for them, and re-layouts: 19.5 us -> 7.89 us
    pallas_call x5 -> x1, Pallas kernels: 107 us -> 80.5 us  [on_device(): pl.pallas_call(functools.partial(block_kernel, slides, count, share), out...]
    transpose x5 -> x0, local copies, waits for them, and re-layouts: 4.03 us -> none  [the longest x1 1.92 us: on_device(): up_term.reshape(channels, blocks, across).transpose(1, 0, 2)]
    concatenate x3 -> x0, other arithmetic: 3.72 us -> none  [the longest x2 3.64 us: halo(): return (jnp.concatenate([above, cells, below, spare], axis=1), *rest)]
    transpose x3 -> x0, other arithmetic: 3.36 us -> none  [halo(): above, below = (above.transpose(1, 0, 2), below.transpose(1, 0, 2))]
    slice x7 -> x0, local copies, waits for them, and re-layouts: 3.05 us -> none  [the longest x4 2.25 us: halo(): operands = [turned[:3], turned[height - 3:]]]
    convert_element_type x4 -> x0, other arithmetic: 2.77 us -> none  [the longest x1 1.17 us: sum_everywhere(): return totals.reshape(-1, across)[:length].astype(jnp.float32)]
    broadcast_in_dim x5 -> x0, local copies, waits for them, and re-layouts: 2.68 us -> none  [the longest x1 1.64 us: on_device(): up_bias[:, None]]
    pallas_call x2 -> x0, local copies, waits for them, and re-layouts: 1.72 us -> none  [on_device(): pl.pallas_call(forward_kernel, out_shape=(jax.ShapeDtypeStruct((channels,...]
where the time goes in v1:
time: 89.5 us; the launch traced here: 89 us
  Pallas kernels  80.5 us (90%)
  local copies, waits for them, and re-layouts  7.89 us (9%)
    pallas_call x1, Pallas kernels, on_device(): pl.pallas_call(functools.partial(block_kernel, slides, count, share), out...  80.5 us
    unnamed x11, local copies, waits for them, and re-layouts  6.44 us

profile of v1, /device:TPU:1, one launch (start us, length us, event | category | flops | bytes accessed | tf_op | source)
XLA Modules:
  0.0 89.0 jit_solution(12378890269400199137)
XLA Ops:
  0.6 1.4 %stack.26.channel_ref = f32[8,192]{1,0:T(8,128)} concatenate(f32[1,192]{1,0:T(1,128)} %bitcast.19, f32[1,192]{1,0:T(1,128)} %bitcast.20, f32[1,192]{1,0:T(1,128)} %bitcast.21, f32[1,192]{1,0:T(1,128)} %bitcast.22, f32[1,192]{1,0:T(1,128)} %bitcast.14, f32[1,192]{1,0:T(1,128)} %bitcast.15, f32[1,192]{1,0:T(1,128)} %bitcast.16, f32[1,192]{1,0:T(1,128)} %bitcast.17), dimensions={0} | concatenate | bytes 12288 | tf_op jit(solution)/shard_map/stack | solution.py:546
  2.1 80.5 %block.1 = (f32[1,4,192]{2,1,0:T(4,128)}, bf16[1,192,32,128]{3,2,1,0:T(8,128)(2,1)}, f32[192,768]{1,0:T(8,128)}, f32[192,768]{1,0:T(8,128)}, f32[49,192]{1,0:T(8,128)}) custom-call(s32[1,32]{1,0:T(1,128)} %order_ref.1, s32[1,1,4]{2,1,0:T(1,128)} %tissue_ref.1, bf16[1,192,32,128]{3,2,1,0:T(8,128)(2,1)} %image_ref.1, bf16[1,4,192]{2,1,0:T(4,128)(2,1)} %tile_ref.1, ...), custom_call_target="tpu_custom_call" | custom-call | tf_op jit(solution)/shard_map/block/pallas_call | solution.py:491
  82.6 1.3 %copy.23 = f32[1,4,192]{2,1,0:T(4,128)} copy(f32[1,4,192]{2,1,0:T(4,128)} %get-tuple-element.20) | data formatting | bytes 6144
  83.8 0.0 copy-start.1
  83.8 0.0 copy-start
  83.8 2.9 %copy.24 = bf16[1,192,32,128]{3,2,1,0:T(8,128)(2,1)} copy(bf16[1,192,32,128]{3,2,1,0:T(8,128)(2,1)} %get-tuple-element.21) | data formatting | bytes 3145728
  86.8 0.0 copy-done.1
  86.8 0.0 copy-start.2
  86.8 0.8 copy.25
  87.6 0.0 copy-done
  87.6 0.8 copy.26
  88.4 0.0 copy-done.2
  88.4 0.6 copy.27
Async XLA Ops:
  83.8 2.9 %copy-start.1 = (f32[192,768]{1,0:T(8,128)S(1)}, f32[192,768]{1,0:T(8,128)}, u32[]{:S(2)}) copy-start(f32[192,768]{1,0:T(8,128)} %get-tuple-element.22) | copy-start | bytes 1769476
  83.8 3.7 %copy-start = (f32[192,768]{1,0:T(8,128)S(1)}, f32[192,768]{1,0:T(8,128)}, u32[]{:S(2)}) copy-start(f32[192,768]{1,0:T(8,128)} %get-tuple-element.13) | copy-start | bytes 1769476
  86.8 1.6 %copy-start.2 = (f32[49,192]{1,0:T(8,128)S(1)}, f32[49,192]{1,0:T(8,128)}, u32[]{:S(2)}) copy-start(f32[49,192]{1,0:T(8,128)} %get-tuple-element.14) | copy-start | bytes 112900

commit v2 on v1

--- a/solution.py
+++ b/solution.py
@@ -14,6 +14,7 @@
 TAPS = 7
 PAD = 3
 EDGE = 4
+OUTER = 8
 LANES = 128
 MESH = pl.DeviceIdType.MESH
 VMEM = pl.BlockSpec(memory_space=pltpu.VMEM)
@@ -98,13 +99,26 @@
     ]
 
 
+def slots(slides, count, share, channels, units):
+    groups, pieces = units // LANES, channels // OUTER
+    found = []
+    for index in range(slides * count * share // OUTER):
+        shard, offset = divmod(index * OUTER, share)
+        group, piece = divmod(index, pieces)
+        side, column = divmod(group, groups)
+        if side > 1:
+            side = None
+        found.append((shard // count, shard % count, offset, side, piece * OUTER, column * LANES))
+    return found
+
+
 def block_kernel(
     slides, count, share, order_ref, tissue_ref, image_ref, tile_ref, taps_in, channel_ref,
     up_ref, up_bias_ref, down_ref,
-    embed_out, grad_out, up_out, down_out, kernel_out,
+    embed_out, grad_out, whole_sum, kernel_out,
     fore_taps, back_taps, halo_out, halo_in, tiles_in, held, sums, hidden_sum, slope_gain,
     up_total, cotangent, scaled_mask, columns, bias, edge_out, edge_in, crossed,
-    part, near, half, far, whole_sum, kpart, knear, khalf, kfar, kwhole,
+    grad_sum, part, near, half, far, kpart, knear, khalf, kfar, kwhole,
     halo_sem, tile_sem, edge_sem, sum_sem, ksum_sem,
 ):
     slide, me = lax.axis_index("slide"), lax.axis_index("rows")
@@ -213,41 +227,109 @@
         sums[pl.ds(c, 1), :] = stacked[TAPS * HALF : TAPS * HALF + 1, :across]
         return carry
 
-    lax.fori_loop(0, channels, conv_channel, 0, unroll=8)
+    lax.fori_loop(0, channels, conv_channel, 0, unroll=16)
 
     blocks = height // ROWS
     edge_copies = edges(edge_out, edge_in, edge_sem)
 
-    def pixels(step, carry):
+    units = hidden_units // 2
+    loss_norm = 1.0 / math.sqrt(slides * count * height * across)
+
+    def start(copies):
+        for copy in copies:
+            copy.start()
+
+    def finish(copies):
+        for copy in copies:
+            copy.wait()
+
+    def add_parts(own, others, number):
+        total = own.astype(F32)
+        for k in range(number):
+            total = total + others(k).astype(F32)
+        return total.astype(BF16)
+
+    def to_slides(source, target, sem, pair, place):
+        return [
+            remote(
+                source.at[peer[0]] if place is None else source.at[place],
+                target.at[k] if place is None else target.at[place],
+                sem.at[pair, k], sem.at[pair + 1, k], peer,
+            )
+            for k, peer in enumerate(across_peers)
+        ]
+
+    def to_rows(source, target, sem, pair, place):
+        return [
+            remote(
+                source.at[peer[1]] if place is None else source.at[place],
+                target.at[k] if place is None else target.at[place],
+                sem.at[pair, k], sem.at[pair + 1, k], peer,
+            )
+            for k, peer in enumerate(along_peers)
+        ]
+
+    stages = []
+    for h in range(2):
+        mine = whole_sum.at[h, slide]
+        stages.append(
+            [
+                to_slides(part.at[h], near.at[h], sum_sem.at[h], 0, None),
+                to_rows(half.at[h], far.at[h], sum_sem.at[h], 2, None),
+                to_rows(mine, mine, sum_sem.at[h], 4, me),
+                to_slides(whole_sum.at[h], whole_sum.at[h], sum_sem.at[h], 6, slide),
+            ]
+        )
+
+    def add_slides(h):
+        finish(stages[h][0])
+        for r in range(count):
+            half[h, r] = add_parts(part[h, slide, r], lambda k: near[h, k, r], slides - 1)
+        start(stages[h][1])
+
+    def add_rows(h):
+        finish(stages[h][1])
+        whole_sum[h, slide, me] = add_parts(half[h, me], lambda k: far[h, k], count - 1)
+        start(stages[h][2])
+
+    def pass_on(h):
+        finish(stages[h][2])
+        start(stages[h][3])
+
+    def wide(cells):
+        return jnp.concatenate([cells] * ROWS, axis=1)
+
+    def pixels(h, step, carry):
         block = jnp.where(step == 0, 0, jnp.where(step == 1, blocks - 1, step - 1))
+        mine = slice(h * units, (h + 1) * units)
 
         def start_of(r):
             return pl.multiple_of((block * ROWS + r + PAD) * channels, 8)
 
-        def wide(ref):
-            return jnp.concatenate([ref[...]] * ROWS, axis=1)
-
         conv = jnp.concatenate([held[pl.ds(start_of(r), channels), :] for r in range(ROWS)], axis=1)
-        conv = conv + wide(conv_bias)
+        conv = conv + wide(conv_bias[...])
         average = jnp.mean(conv, axis=0, keepdims=True)
         centered = conv - average
         variance = jnp.mean(centered * centered, axis=0, keepdims=True)
         reciprocal = lax.rsqrt(variance + 1e-06)
         standard = centered * reciprocal
-        normed = (standard * wide(gain) + wide(norm_bias)).astype(BF16)
-        act = dot(up_ref[...], normed, (0, 0)) + wide(bias)
+        normed = (standard * wide(gain[...]) + wide(norm_bias[...])).astype(BF16)
+        act = dot(up_ref[:, mine], normed, (0, 0)) + wide(bias[mine])
         cumulative = 0.5 + 0.5 * lax.erf(act * 0.7071067811865476)
         hidden = (act * cumulative).astype(BF16).astype(F32)
-        total = hidden_sum[...]
+        total = hidden_sum[mine]
         for r in range(ROWS):
             total = total + hidden[:, r * across : (r + 1) * across]
-        hidden_sum[...] = total
+        hidden_sum[mine] = total
         density = jnp.exp(-0.5 * act * act) * 0.3989422804014327
         slope = cumulative + act * density
-        grad_act = (wide(slope_gain) * slope).astype(BF16)
-        grad_normed = dot(up_ref[...], grad_act, (1, 0))
-        up_total[...] += dot(normed, grad_act, (1, 1))
-        grad_standard = grad_normed * wide(gain)
+        grad_act = (wide(slope_gain[mine]) * slope).astype(BF16)
+        grad_normed = dot(up_ref[:, mine], grad_act, (1, 0))
+        up_total[:, mine] += dot(normed, grad_act, (1, 1))
+        if h == 0:
+            grad_sum[block] = grad_normed
+            return carry
+        grad_standard = (grad_sum[block] + grad_normed) * wide(gain[...])
         first = jnp.mean(grad_standard, axis=0, keepdims=True)
         second = jnp.mean(grad_standard * standard, axis=0, keepdims=True)
         grad_conv = reciprocal * (grad_standard - first - standard * second)
@@ -263,18 +345,32 @@
                 edge_out[1, r] = held[low : low + channels, :].astype(BF16)
             start_edges(edge_copies)
 
+        @pl.when(step == blocks // 2)
+        def _():
+            add_slides(0)
+
         return carry
 
-    lax.fori_loop(0, blocks, pixels, 0)
-
-    loss_norm = 1.0 / math.sqrt(slides * count * height * across)
-    total_parts = split(hidden_sum[...], 2)
+    grad_branch = (scaled_mask[...] * cotangent[...]).astype(BF16)
     branch = jnp.zeros((channels, across), F32)
-    down = jnp.zeros((channels, hidden_units), F32)
-    grad_branch = (scaled_mask[...] * cotangent[...]).astype(BF16)
-    for piece in total_parts:
-        branch += dot(down_ref[...], piece, (1, 0))
-        down += dot(grad_branch, piece, (1, 1))
+    for h in range(2):
+        lax.fori_loop(0, blocks, functools.partial(pixels, h), 0)
+        mine = slice(h * units, (h + 1) * units)
+        down = jnp.zeros((channels, units), F32)
+        for piece in split(hidden_sum[mine], 2):
+            branch += dot(down_ref[:, mine], piece, (1, 0))
+            down += dot(grad_branch, piece, (1, 1))
+        for s, r, offset, side, low, at in slots(slides, count, share, channels, units):
+            if side is None:
+                values = jnp.zeros((OUTER, LANES), F32)
+            elif side == 0:
+                values = up_total[low : low + OUTER, h * units + at : h * units + at + LANES]
+            else:
+                values = down[low : low + OUTER, at : at + LANES]
+            part[h, s, r, offset : offset + OUTER, :] = (values * loss_norm).astype(BF16)
+        start(stages[h][0])
+
+    add_rows(0)
     embed = sums[...] + scaled_mask[...] * (branch + height * down_bias[...])
     tile_of = lax.div(lax.broadcasted_iota(jnp.int32, (tiles_here, across), 1), TILE)
     picks = jnp.where(
@@ -284,51 +380,6 @@
     for piece in split(embed, 3):
         embedded += dot(picks, piece, (1, 1))
     embed_out[0] = embedded * (1.0 / (height * TILE))
-
-    groups = hidden_units // LANES
-    pieces = channels // HALF
-
-    def slot_of(index):
-        shard, offset = divmod(index * HALF, share)
-        return shard // count, shard % count, offset
-
-    used = 2 * groups * pieces
-    for index in range(slides * count * share // HALF):
-        s, r, offset = slot_of(index)
-        if index >= used:
-            part[s, r, offset : offset + HALF, :] = jnp.zeros((HALF, LANES), BF16)
-            continue
-        group, piece = divmod(index, pieces)
-        low = piece * HALF
-        if group < groups:
-            values = up_total[low : low + HALF, group * LANES : (group + 1) * LANES]
-        else:
-            at = (group - groups) * LANES
-            values = down[low : low + HALF, at : at + LANES]
-        part[s, r, offset : offset + HALF, :] = (values * loss_norm).astype(BF16)
-
-    def sum_slides(part_ref, near_ref, sem):
-        return [
-            remote(part_ref.at[peer[0]], near_ref.at[k], sem.at[0, k], sem.at[1, k], peer)
-            for k, peer in enumerate(across_peers)
-        ]
-
-    def sum_rows(half_ref, far_ref, sem):
-        return [
-            remote(half_ref.at[peer[1]], far_ref.at[k], sem.at[2, k], sem.at[3, k], peer)
-            for k, peer in enumerate(along_peers)
-        ]
-
-    def start(copies):
-        for copy in copies:
-            copy.start()
-
-    def finish(copies):
-        for copy in copies:
-            copy.wait()
-
-    first = sum_slides(part, near, sum_sem)
-    start(first)
 
     band_row = lax.broadcasted_iota(jnp.int32, (2 * HALF, LANES), 0) + 8
     band_lane = lax.broadcasted_iota(jnp.int32, (2 * HALF, LANES), 1)
@@ -361,7 +412,7 @@
         crossed[pl.ds(pl.multiple_of(c * 8, 8), 8), :] = total
         return carry
 
-    lax.fori_loop(0, channels, cross_channel, 0, unroll=8)
+    lax.fori_loop(0, channels, cross_channel, 0, unroll=16)
 
     kernel_term = crossed[pl.ds(0, channels, stride=8), :]
     for k in range(1, 8):
@@ -372,20 +423,17 @@
     for k in range(count):
         low = k * step_rows
         kpart[k, :step_rows, :] = kernel_term[low : low + step_rows].astype(BF16)
-    kfirst = [
-        remote(kpart, knear.at[k], ksum_sem.at[0, k], ksum_sem.at[1, k], peer)
-        for k, peer in enumerate(across_peers)
+    kstages = [
+        [
+            remote(kpart, knear.at[k], ksum_sem.at[0, k], ksum_sem.at[1, k], peer)
+            for k, peer in enumerate(across_peers)
+        ],
+        to_rows(khalf, kfar, ksum_sem, 2, None),
+        to_rows(kwhole, kwhole, ksum_sem, 4, me),
     ]
-    start(kfirst)
-
-    finish(first)
-    for r in range(count):
-        total = part[slide, r].astype(F32)
-        for k in range(slides - 1):
-            total = total + near[k, r].astype(F32)
-        half[r] = total.astype(BF16)
-    second = sum_rows(half, far, sum_sem)
-    start(second)
+    start(kstages[0])
+    add_slides(1)
+    pass_on(0)
 
     finish_edges(edge_copies)
     for r in range(PAD):
@@ -405,61 +453,43 @@
     third_of = channels // 3
     lax.fori_loop(0, third_of, back_channel, 0, unroll=8)
 
-    finish(kfirst)
+    finish(kstages[0])
     for r in range(count):
-        total = kpart[r].astype(F32)
-        for k in range(slides - 1):
-            total = total + knear[k, r].astype(F32)
-        khalf[r] = total.astype(BF16)
-    ksecond = sum_rows(khalf, kfar, ksum_sem)
-    start(ksecond)
-    finish(second)
-    total = half[me].astype(F32)
-    for k in range(count - 1):
-        total = total + far[k].astype(F32)
-    whole_sum[slide, me] = total.astype(BF16)
-    third = [
-        remote(whole_sum.at[slide, me], whole_sum.at[slide, me], sum_sem.at[4, k], sum_sem.at[5, k], peer)
-        for k, peer in enumerate(along_peers)
-    ]
-    start(third)
+        khalf[r] = add_parts(kpart[r], lambda k: knear[k, r], slides - 1)
+    start(kstages[1])
+    add_rows(1)
 
     lax.fori_loop(third_of, 2 * third_of, back_channel, 0, unroll=8)
 
-    finish(ksecond)
-    total = khalf[me].astype(F32)
-    for k in range(count - 1):
-        total = total + kfar[k].astype(F32)
-    kwhole[me] = total.astype(BF16)
-    kthird = [
-        remote(kwhole.at[me], kwhole.at[me], ksum_sem.at[4, k], ksum_sem.at[5, k], peer)
-        for k, peer in enumerate(along_peers)
-    ]
-    start(kthird)
-    finish(third)
-    fourth = [
-        remote(whole_sum.at[slide], whole_sum.at[slide], sum_sem.at[6, k], sum_sem.at[7, k], peer)
-        for k, peer in enumerate(across_peers)
-    ]
-    start(fourth)
+    finish(kstages[1])
+    kwhole[me] = add_parts(khalf[me], lambda k: kfar[k], count - 1)
+    start(kstages[2])
+    pass_on(1)
 
     lax.fori_loop(2 * third_of, channels, back_channel, 0, unroll=8)
 
-    finish(kthird)
+    finish(kstages[2])
     rows = jnp.concatenate([kwhole[k, :step_rows, :].astype(F32) for k in range(count)], axis=0)
     tap = lax.broadcasted_iota(jnp.int32, (TAPS * TAPS, LANES), 0)
     at = HALF * lax.rem(tap, TAPS) - lax.div(tap, TAPS) - (HALF - PAD) + 8 + LANES
     at = lax.rem(at, LANES) == lax.broadcasted_iota(jnp.int32, (TAPS * TAPS, LANES), 1)
     kernel_out[...] = dot(jnp.where(at, 1.0, 0.0).astype(BF16), rows.astype(BF16), (1, 1))
-    finish(fourth)
-    for index in range(used):
-        s, r, offset = slot_of(index)
-        group, piece = divmod(index, pieces)
-        low = piece * HALF
-        values = whole_sum[s, r, offset : offset + HALF, :].astype(F32)
-        target = up_out if group < groups else down_out
-        at = group % groups * LANES
-        target[low : low + HALF, at : at + LANES] = values
+    finish(stages[0][3])
+    finish(stages[1][3])
+
+
+def spread_kernel(grad_ref, whole_ref, grad_out, up_out, down_out):
+    grad_out[...] = grad_ref[...]
+    halves, slides, count, share, _ = whole_ref.shape
+    channels, hidden_units = up_out.shape
+    units = hidden_units // halves
+    for h in range(halves):
+        for s, r, offset, side, low, at in slots(slides, count, share, channels, units):
+            if side is None:
+                continue
+            target = (up_out, down_out)[side]
+            values = whole_ref[h, s, r, offset : offset + OUTER, :].astype(F32)
+            target[low : low + OUTER, h * units + at : h * units + at + LANES] = values
 
 
 def on_device(
@@ -481,24 +511,23 @@
     hidden_units = up_weight.shape[1]
     tiles_here = across // TILE
     slides, count = lax.axis_size("slide"), lax.axis_size("rows")
-    entries = 2 * channels * hidden_units // LANES
-    share = HALF * pl.cdiv(entries, HALF * slides * count)
+    entries = channels * hidden_units // LANES
+    share = OUTER * pl.cdiv(entries, OUTER * slides * count)
     kshare = HALF * pl.cdiv(channels // count, HALF)
-    span = (slides, count, share, LANES)
+    span = (2, slides, count, share, LANES)
     kspan = (count, kshare, LANES)
     most = max(slides, count) - 1
     dma = pltpu.SemaphoreType.DMA
-    embedding, input_grad, grad_up, grad_down, grad_kernel = pl.pallas_call(
+    embedding, input_grad, whole_sum, grad_kernel = pl.pallas_call(
         functools.partial(block_kernel, slides, count, share),
         out_shape=(
             jax.ShapeDtypeStruct((1, tiles_here, channels), F32),
             jax.ShapeDtypeStruct(features.shape, BF16),
-            jax.ShapeDtypeStruct((channels, hidden_units), F32),
-            jax.ShapeDtypeStruct((channels, hidden_units), F32),
+            jax.ShapeDtypeStruct(span, BF16),
             jax.ShapeDtypeStruct((TAPS * TAPS, channels), F32),
         ),
         in_specs=[SMEM, SMEM] + [VMEM] * 7,
-        out_specs=(VMEM,) * 5,
+        out_specs=(VMEM,) * 4,
         scratch_shapes=[
             pltpu.VMEM((TAPS, channels, LANES), F32),
             pltpu.VMEM((TAPS, channels, LANES), F32),
@@ -517,11 +546,11 @@
             pltpu.VMEM((2, PAD, channels, across), BF16),
             pltpu.VMEM((2, PAD, channels, across), BF16),
             pltpu.VMEM((channels * 8, LANES), F32),
+            pltpu.VMEM((height // ROWS, channels, ROWS * across), F32),
             pltpu.VMEM(span, BF16),
-            pltpu.VMEM((slides - 1,) + span[1:], BF16),
-            pltpu.VMEM(span[1:], BF16),
-            pltpu.VMEM((count - 1,) + span[2:], BF16),
-            pltpu.VMEM(span, BF16),
+            pltpu.VMEM((2, slides - 1) + span[2:], BF16),
+            pltpu.VMEM((2,) + span[2:], BF16),
+            pltpu.VMEM((2, count - 1) + span[3:], BF16),
             pltpu.VMEM(kspan, BF16),
             pltpu.VMEM((slides - 1,) + kspan, BF16),
             pltpu.VMEM(kspan, BF16),
@@ -530,7 +559,7 @@
             dma((4,)),
             dma((2, most)),
             dma((4,)),
-            dma((8, most)),
+            dma((2, 8, most)),
             dma((6, most)),
         ],
         compiler_params=pltpu.CompilerParams(
@@ -548,6 +577,17 @@
         up_bias.reshape(-1, LANES),
         down_weight.T,
     )
+    input_grad, grad_up, grad_down = pl.pallas_call(
+        spread_kernel,
+        out_shape=(
+            jax.ShapeDtypeStruct(features.shape, BF16),
+            jax.ShapeDtypeStruct((channels, hidden_units), F32),
+            jax.ShapeDtypeStruct((channels, hidden_units), F32),
+        ),
+        in_specs=[VMEM] * 2,
+        out_specs=(VMEM,) * 3,
+        name="spread",
+    )(input_grad, whole_sum)
     return embedding, input_grad, grad_up, grad_down.T, grad_kernel.T
 
 

time: 89.5 us -> 82 us (0.916)
  local copies, waits for them, and re-layouts: 7.89 us -> 2.67 us
  Pallas kernels: 80.5 us -> 78.5 us
    unnamed x11 -> x6, local copies, waits for them, and re-layouts: 6.44 us -> 1.22 us
    pallas_call x1, Pallas kernels: 80.5 us -> 75.3 us  [on_device(): pl.pallas_call(functools.partial(block_kernel, slides, count, share), out...]
    pallas_call x0 -> x1, Pallas kernels: none -> 3.15 us  [on_device(): pl.pallas_call(spread_kernel, out_shape=(jax.ShapeDtypeStruct(features.sh...]
where the time goes in v2:
time: 82 us; the launch traced here: 81.8 us
  Pallas kernels  78.5 us (96%)
  local copies, waits for them, and re-layouts  2.67 us (3%)
    pallas_call x1, Pallas kernels, on_device(): pl.pallas_call(functools.partial(block_kernel, slides, count, share), out...  75.3 us
    pallas_call x1, Pallas kernels, on_device(): pl.pallas_call(spread_kernel, out_shape=(jax.ShapeDtypeStruct(features.sh...  3.15 us

profile of v2, /device:TPU:1, one launch (start us, length us, event | category | flops | bytes accessed | tf_op | source)
XLA Modules:
  0.0 81.8 jit_solution(6691327637039656301)
XLA Ops:
  0.6 1.4 %stack.26.channel_ref = f32[8,192]{1,0:T(8,128)} concatenate(f32[1,192]{1,0:T(1,128)} %bitcast.18, f32[1,192]{1,0:T(1,128)} %bitcast.19, f32[1,192]{1,0:T(1,128)} %bitcast.20, f32[1,192]{1,0:T(1,128)} %bitcast.21, f32[1,192]{1,0:T(1,128)} %bitcast.13, f32[1,192]{1,0:T(1,128)} %bitcast.14, f32[1,192]{1,0:T(1,128)} %bitcast.15, f32[1,192]{1,0:T(1,128)} %bitcast.16), dimensions={0} | concatenate | bytes 12288 | tf_op jit(solution)/shard_map/stack | solution.py:575
  2.1 75.3 %block.1 = (f32[1,4,192]{2,1,0:T(4,128)}, bf16[1,192,32,128]{3,2,1,0:T(8,128)(2,1)}, bf16[2,4,8,40,128]{4,3,2,1,0:T(8,128)(2,1)}, f32[49,192]{1,0:T(8,128)}) custom-call(s32[1,32]{1,0:T(1,128)} %order_ref.1, s32[1,1,4]{2,1,0:T(1,128)} %tissue_ref.1, bf16[1,192,32,128]{3,2,1,0:T(8,128)(2,1)} %image_ref.1, bf16[1,4,192]{2,1,0:T(4,128)(2,1)} %tile_ref.1, ...), custom_call_target="tpu_custom_call" | custom-call | tf_op jit(solution)/shard_map/block/pallas_call | solution.py:521
  77.4 0.0 copy-start.1
  77.4 0.0 copy-start
  77.4 3.2 %spread.1 = (bf16[1,192,32,128]{3,2,1,0:T(8,128)(2,1)}, f32[192,768]{1,0:T(8,128)}, f32[192,768]{1,0:T(8,128)}) custom-call(bf16[1,192,32,128]{3,2,1,0:T(8,128)(2,1)} %get-tuple-element.13.grad_ref, bf16[2,4,8,40,128]{4,3,2,1,0:T(8,128)(2,1)} %get-tuple-element.14.whole_ref), custom_call_target="tpu_custom_call" | custom-call | tf_op jit(solution)/shard_map/spread/pallas_call | solution.py:580
  80.6 0.0 copy-done.1
  80.6 0.6 copy.20
  81.2 0.0 copy-done
  81.2 0.6 copy.21
Async XLA Ops:
  77.4 3.2 %copy-start.1 = (f32[1,4,192]{2,1,0:T(4,128)S(1)}, f32[1,4,192]{2,1,0:T(4,128)}, u32[]{:S(2)}) copy-start(f32[1,4,192]{2,1,0:T(4,128)} %get-tuple-element.24) | copy-start | bytes 9220
  77.4 3.8 %copy-start = (f32[49,192]{1,0:T(8,128)S(1)}, f32[49,192]{1,0:T(8,128)}, u32[]{:S(2)}) copy-start(f32[49,192]{1,0:T(8,128)} %get-tuple-element.18) | copy-start | bytes 112900
